TPU v7x, 1024 devices: a whole 4x8x16 slice. The times are simulated.
1024 devices in a mesh: dp: 8 (over y), expert: 64 (over z, x), tensor: 2 (over core).
Axes of the slice: x: 4, y: 8, z: 16, core: 2. Of those that a mesh axis runs over, the one named last changes fastest.
Arguments:
- out_grad: bfloat16 [65536, 3584], P(('dp', 'expert'), 'tensor'), may hold values from -6 to 6
- routes: int32 [65536, 8], P(('dp', 'expert')), may hold values from 0 to 255, all different within a row; in each aligned block of 128 rows (0 to 127, 128 to 255, ...) at most 5 rows name the same one
- probs: float32 [65536, 8], P(('dp', 'expert')), may hold values from 0.1 to 1
- gate_pre: bfloat16 [8, 64, 320, 1024], P('dp', 'expert', None, 'tensor'), may hold values from -8 to 8
- up_pre: bfloat16 [8, 64, 320, 1024], P('dp', 'expert', None, 'tensor'), may hold values from -6 to 6
- gate_weight: bfloat16 [64, 3584, 1024], P('expert', None, 'tensor'), may hold values from -0.09375 to 0.09375
- up_weight: bfloat16 [64, 3584, 1024], P('expert', None, 'tensor'), may hold values from -0.09375 to 0.09375
- down_weight: bfloat16 [64, 1024, 3584], P('expert', 'tensor', 'dp'), may hold values from -0.1875 to 0.1875
Outputs:
- input_grad: bfloat16 [65536, 3584], P(('dp', 'expert'), 'tensor')
Inputs may be any that keep to these rules, and one draw needn't show every extreme that they name: Each row names 8 different experts. In the 128 rows of one device no expert is named more than 5 times. Ids below 64 are the experts held here, expert e at index e of expert; routes to other ids leave no slot.
All inputs are finite; a program needn't handle non-finite values.
Results may differ from a plain program's by a relative error of at most 0.0072.
Values may be sent and summed in bfloat16 or wider, within the bound.
A program may use at most 64 MiB of HBM per device.

v0:
```python
import jax
import jax.numpy as jnp
from jax import lax
from jax.sharding import PartitionSpec as P

CAP = 5


def cut_along(x, dim, devices):
    before, after = (x.shape[:dim], x.shape[dim + 1 :])
    return jnp.moveaxis(x.reshape(*before, devices, -1, *after), dim, 0)


def cut_rows(length, count):
    unit = 8 if length >= 8 * count else 1
    return [length // unit * k // count * unit for k in range(1, count)]


def in_order(parts, dim):
    parts = jnp.moveaxis(parts, 0, dim)
    dims = parts.shape
    return parts.reshape(*dims[:dim], dims[dim] * dims[dim + 1], *dims[dim + 2 :])


def cut_exchange(x, axis, pieces, split_dim, concat_dim):
    parts = cut_along(x, split_dim, lax.axis_size(axis))
    split_at = max(range(1, max(2, parts.ndim - 1)), key=lambda d: parts.shape[d])
    outs = []
    for piece in jnp.split(parts, cut_rows(parts.shape[split_at], pieces), axis=split_at):
        if piece.size:
            outs.append(lax.all_to_all(piece, axis, split_axis=0, concat_axis=0, tiled=True))
    return in_order(jnp.concatenate(outs, axis=split_at), concat_dim)


def sent_to_all(x, axis):
    copies = jnp.broadcast_to(x, (lax.axis_size(axis), *x.shape))
    return lax.all_to_all(copies, axis, split_axis=0, concat_axis=0, tiled=True)


def collect(x, axis, dim):
    return in_order(sent_to_all(x, axis), dim)


def sent_and_summed(x, axis, dim):
    devices = lax.axis_size(axis)
    parts = lax.all_to_all(cut_along(x, dim, devices), axis, 0, 0, tiled=True)
    return jnp.sum(parts.astype(jnp.float32), axis=0)


def slot_tables(block_routes, block_probs, experts, capacity):
    expert_ids = jnp.arange(experts, dtype=jnp.int32)
    matches = block_routes[:, :, None] == expert_ids[None, None, :]
    picked = jnp.sum(matches.astype(jnp.int32), axis=1)
    weight = jnp.sum(jnp.where(matches, block_probs[:, :, None], jnp.float32(0.0)), axis=1)
    before = jnp.cumsum(picked, axis=0) - picked
    rank_ids = jnp.arange(capacity, dtype=jnp.int32)
    select = (picked.T[:, None, :] == 1) & (before.T[:, None, :] == rank_ids[None, :, None])
    slot_scale = jnp.sum(jnp.where(select, weight.T[:, None, :], jnp.float32(0.0)), axis=2)
    return (select, slot_scale)


def local(out_grad, routes, probs, gate_pre, up_pre, gate_weight, up_weight, down_weight):
    experts = lax.axis_size("expert")
    select, slot_scale = slot_tables(routes, probs, experts, CAP)
    slot_count = experts * CAP
    slot_table = select.reshape(slot_count, -1).astype(jnp.bfloat16)
    picked_rows = jnp.dot(slot_table, out_grad, preferred_element_type=jnp.float32)
    outgoing = (
        (slot_scale.reshape(-1, 1) * picked_rows).astype(jnp.bfloat16).reshape(experts, CAP, -1)
    )
    arrived = cut_exchange(outgoing, "expert", 2, 0, 0)
    arrived_rows = arrived.reshape(slot_count, -1)
    gathered = collect(arrived_rows, "tensor", 1)
    down_local = down_weight[0]
    hidden_grad = lax.dot_general(
        gathered,
        lax.all_gather(down_local, "dp", axis=1, tiled=True),
        (((1,), (1,)), ((), ())),
        preferred_element_type=jnp.float32,
    )
    gate_act = gate_pre[0, 0].astype(jnp.float32)
    up_act = up_pre[0, 0].astype(jnp.float32)
    sigmoid_gate = jax.nn.sigmoid(gate_act)
    activated = gate_act * sigmoid_gate
    derivative = sigmoid_gate * (1.0 + gate_act * (1.0 - sigmoid_gate))
    gate_grad = (hidden_grad * up_act * derivative).astype(jnp.bfloat16)
    up_grad = (hidden_grad * activated).astype(jnp.bfloat16)
    partial_value = lax.dot_general(
        gate_grad, gate_weight[0], (((1,), (1,)), ((), ())), preferred_element_type=jnp.float32
    )
    partial_value = partial_value + lax.dot_general(
        up_grad, up_weight[0], (((1,), (1,)), ((), ())), preferred_element_type=jnp.float32
    )
    summed = sent_and_summed(partial_value.astype(jnp.bfloat16), "tensor", 1)
    slot_grad = summed.astype(jnp.bfloat16).reshape(experts, CAP, -1)
    returned = cut_exchange(slot_grad, "expert", 2, 0, 0).reshape(slot_count, -1)
    combined = lax.dot_general(
        slot_table, returned, (((0,), (0,)), ((), ())), preferred_element_type=jnp.float32
    )
    return combined.astype(jnp.bfloat16)


def solution(mesh):
    placed = (
        P(("dp", "expert"), "tensor"),
        P(("dp", "expert"), None),
        P(("dp", "expert"), None),
        P("dp", "expert", None, "tensor"),
        P("dp", "expert", None, "tensor"),
        P("expert", None, "tensor"),
        P("expert", None, "tensor"),
        P("expert", "tensor", "dp"),
    )
    return jax.shard_map(
        local, mesh=mesh, in_specs=placed, out_specs=P(("dp", "expert"), "tensor"), check_vma=False
    )
```

profile of v0, /device:TPU:1, one launch (start us, length us, event | category | flops | bytes accessed | tf_op | source)
XLA Modules:
  0.0 243.7 jit_solution(16095679127700853854)
XLA Ops:
  6.5 0.0 copy-start
  6.5 0.0 all-gather.3.cloned.1.call-start
  6.5 0.7 all-gather.3.cloned.1.call-update
  7.3 0.7 convert_reduce_fusion
  8.0 0.1 copy.27
  8.1 0.2 reduce_window_sum.11
  8.3 0.1 copy.29
  8.3 0.8 select_reduce_fusion.1
  9.1 0.1 select_reduce_fusion
  9.3 0.1 mul.28
  9.6 0.1 eq.65
  9.7 0.0 copy-done
  9.7 0.5 fusion.6
  10.2 0.5 reshape_reshape.12
  10.7 1.1 slice_bitcast_fusion.3
  11.8 23.0 %all-to-all-start = ((bf16[64,1,2,1792]{3,2,1,0:T(2,128)(2,1)}), bf16[64,1,2,1792]{3,2,1,0:T(2,128)(2,1)}, u32[]{:S(2)}, u32[]{:S(2)}) async-start(bf16[64,1,2,1792]{3,2,1,0:T(2,128)(2,1)} %slice_bitcast_fusion.3), calls=%async_computation | async-start | bytes 917504 | tf_op jit(solution)/shard_map/all_to_all | solution.py:31
  34.8 0.5 slice_bitcast_fusion.1
  35.3 26.6 %all-to-all-done = bf16[64,1,2,1792]{3,2,1,0:T(2,128)(2,1)} async-done(((bf16[64,1,2,1792]{3,2,1,0:T(2,128)(2,1)}), bf16[64,1,2,1792]{3,2,1,0:T(2,128)(2,1)}, u32[]{:S(2)}, u32[]{:S(2)}) %all-to-all-start) | async-done | bytes 458784 | tf_op jit(solution)/shard_map/all_to_all | solution.py:31
  61.9 54.0 %all_to_all.30 = bf16[64,1,3,1792]{3,2,1,0:T(4,128)(2,1)S(1)} all-to-all(bf16[64,1,3,1792]{3,2,1,0:T(4,128)(2,1)S(1)} %slice_bitcast_fusion.1), channel_id=1, replica_groups=mesh['dp'=8,'expert'=64,'tensor'=2] {'expert'}, dimensions={0} | all-to-all | bytes 1376256 | tf_op jit(solution)/shard_map/all_to_all | solution.py:31
  115.9 1.9 pad_maximum_fusion
  117.8 0.5 reshape_reshape.13
  118.4 0.1 broadcast_in_dim.38
  118.5 9.6 %all_to_all.31 = bf16[2,320,1792]{2,1,0:T(8,128)(2,1)S(1)} all-to-all(bf16[2,320,1792]{2,1,0:T(8,128)(2,1)S(1)} %broadcast_in_dim.38), channel_id=1, replica_groups=mesh['dp'=8,'expert'=64,'tensor'=2] {'tensor'}, dimensions={0} | all-to-all | bytes 4587520 | tf_op jit(solution)/shard_map/all_to_all | solution.py:37
  128.1 0.2 copy.37
  128.3 0.0 all-gather.3.cloned.1.call-done
  128.3 0.0 copy-start.1
  128.3 0.0 copy-start.3
  128.3 0.0 copy-start.4
  128.3 3.5 %fusion.4 = f32[320,512]{1,0:T(8,128)S(1)} fusion(bf16[320,3584]{1,0:T(8,128)(2,1)S(1)} %bitcast.55, bf16[1,512,3584]{1,2,0:T(8,128)(2,1)} %all-gather.3.cloned.1.call-done), kind=kOutput, calls=%fused_computation.5 | convolution fusion | flops 1174405120 | bytes 6619136 | tf_op jit(solution)/shard_map/dot_general | solution.py:75
  131.9 0.0 copy-done.1
  131.9 0.0 copy-done.3
  131.9 0.0 copy-done.4
  131.9 0.0 copy-start.2
  131.9 1.5 fusion.2
  133.4 0.5 copy-done.2
  133.9 1.4 fusion
  135.4 0.1 copy.39
  135.5 5.6 %all_to_all.32 = bf16[2,320,1792]{2,1,0:T(8,128)(2,1)S(1)} all-to-all(bf16[2,320,1792]{2,1,0:T(8,128)(2,1)S(1)} %bitcast.54), channel_id=1, replica_groups=mesh['dp'=8,'expert'=64,'tensor'=2] {'tensor'}, dimensions={0} | all-to-all | bytes 4587520 | tf_op jit(solution)/shard_map/all_to_all | solution.py:46
  141.1 1.7 reduce_sum.42
  142.8 2.3 reshape_reshape.14
  145.1 1.1 slice_bitcast_fusion.2
  146.2 6.0 %all-to-all-start.4 = ((bf16[64,1,2,1792]{3,2,1,0:T(2,128)(2,1)}), bf16[64,1,2,1792]{3,2,1,0:T(2,128)(2,1)}, u32[]{:S(2)}, u32[]{:S(2)}) async-start(bf16[64,1,2,1792]{3,2,1,0:T(2,128)(2,1)} %slice_bitcast_fusion.2), calls=%async_computation.4 | async-start | bytes 917504 | tf_op jit(solution)/shard_map/all_to_all | solution.py:31
  152.2 1.4 slice_bitcast_fusion
  153.6 26.9 %all-to-all-done.4 = bf16[64,1,2,1792]{3,2,1,0:T(2,128)(2,1)} async-done(((bf16[64,1,2,1792]{3,2,1,0:T(2,128)(2,1)}), bf16[64,1,2,1792]{3,2,1,0:T(2,128)(2,1)}, u32[]{:S(2)}, u32[]{:S(2)}) %all-to-all-start.4) | async-done | bytes 458784 | tf_op jit(solution)/shard_map/all_to_all | solution.py:31
  180.5 6.5 %all-to-all-start.5 = ((bf16[64,1,3,1792]{3,2,1,0:T(4,128)(2,1)}), bf16[64,1,3,1792]{3,2,1,0:T(4,128)(2,1)S(1)}, u32[]{:S(2)}, u32[]{:S(2)}) async-start(bf16[64,1,3,1792]{3,2,1,0:T(4,128)(2,1)} %slice_bitcast_fusion), calls=%async_computation.5 | async-start | bytes 1835008 | tf_op jit(solution)/shard_map/all_to_all | solution.py:31
  187.0 0.1 fusion.23
  187.1 46.1 %all-to-all-done.5 = bf16[64,1,3,1792]{3,2,1,0:T(4,128)(2,1)S(1)} async-done(((bf16[64,1,3,1792]{3,2,1,0:T(4,128)(2,1)}), bf16[64,1,3,1792]{3,2,1,0:T(4,128)(2,1)S(1)}, u32[]{:S(2)}, u32[]{:S(2)}) %all-to-all-start.5) | async-done | bytes 688160 | tf_op jit(solution)/shard_map/all_to_all | solution.py:31
  233.2 1.9 pad_maximum_fusion.1
  235.2 0.5 reshape_reshape.15
  235.7 1.2 convolution_convert_fusion
  (8 shorter events, 0.2 us)
Async XLA Ops:
  6.5 3.2 %copy-start = (bf16[128,1792]{1,0:T(8,128)(2,1)S(1)}, bf16[128,1792]{1,0:T(8,128)(2,1)}, u32[]{:S(2)}) copy-start(bf16[128,1792]{1,0:T(8,128)(2,1)} %param.8) | copy-start | bytes 1376260
  6.5 121.8 %all-gather.3.cloned.1.call-start = ((), (), s32[]{:S(2)}) async-start(), calls=%async_computation.6 | async-start | bytes 4128768 | tf_op jit(solution)/shard_map/all_gather | solution.py:77
  11.8 50.1 %all-to-all-start = ((bf16[64,1,2,1792]{3,2,1,0:T(2,128)(2,1)}), bf16[64,1,2,1792]{3,2,1,0:T(2,128)(2,1)}, u32[]{:S(2)}, u32[]{:S(2)}) async-start(bf16[64,1,2,1792]{3,2,1,0:T(2,128)(2,1)} %slice_bitcast_fusion.3), calls=%async_computation | async-start | bytes 917504 | tf_op jit(solution)/shard_map/all_to_all | solution.py:31
  128.3 3.6 %copy-start.1 = (bf16[1,3584,512]{2,1,0:T(8,128)(2,1)S(1)}, bf16[1,3584,512]{2,1,0:T(8,128)(2,1)}, u32[]{:S(2)}) copy-start(bf16[1,3584,512]{2,1,0:T(8,128)(2,1)} %param.13) | copy-start | bytes 11010052
  128.3 3.6 %copy-start.3 = (bf16[1,1,320,512]{3,2,1,0:T(8,128)(2,1)S(1)}, bf16[1,1,320,512]{3,2,1,0:T(8,128)(2,1)}, u32[]{:S(2)}) copy-start(bf16[1,1,320,512]{3,2,1,0:T(8,128)(2,1)} %param.11) | copy-start | bytes 983044
  128.3 3.6 %copy-start.4 = (bf16[1,1,320,512]{3,2,1,0:T(8,128)(2,1)S(1)}, bf16[1,1,320,512]{3,2,1,0:T(8,128)(2,1)}, u32[]{:S(2)}) copy-start(bf16[1,1,320,512]{3,2,1,0:T(8,128)(2,1)} %param.12) | copy-start | bytes 983044
  131.9 2.0 copy-start.2
  146.2 34.3 %all-to-all-start.4 = ((bf16[64,1,2,1792]{3,2,1,0:T(2,128)(2,1)}), bf16[64,1,2,1792]{3,2,1,0:T(2,128)(2,1)}, u32[]{:S(2)}, u32[]{:S(2)}) async-start(bf16[64,1,2,1792]{3,2,1,0:T(2,128)(2,1)} %slice_bitcast_fusion.2), calls=%async_computation.4 | async-start | bytes 917504 | tf_op jit(solution)/shard_map/all_to_all | solution.py:31
  180.5 52.8 %all-to-all-start.5 = ((bf16[64,1,3,1792]{3,2,1,0:T(4,128)(2,1)}), bf16[64,1,3,1792]{3,2,1,0:T(4,128)(2,1)S(1)}, u32[]{:S(2)}, u32[]{:S(2)}) async-start(bf16[64,1,3,1792]{3,2,1,0:T(4,128)(2,1)} %slice_bitcast_fusion), calls=%async_computation.5 | async-start | bytes 1835008 | tf_op jit(solution)/shard_map/all_to_all | solution.py:31
Sparse Core Ops, SparseCore 0:
  10.0 65.8 all-gather.2
where the time goes:
time: 247 us; the launch traced here: 244 us
  waiting for transfers between devices  100 us (40%)
  blocking collectives  69.1 us (28%)
  starting transfers between devices  35.5 us (14%)
  between operations  13.7 us (6%)
  local copies, waits for them, and re-layouts  9.49 us (4%)
  matrix products  8.17 us (3%)
  other arithmetic  7.41 us (3%)
    all_to_all x3, waiting for transfers between devices, cut_exchange(): lax.all_to_all(piece, axis, split_axis=0, concat_axis=0, tiled=True)  99.6 us
    all_to_all x1, blocking collectives, cut_exchange(): lax.all_to_all(piece, axis, split_axis=0, concat_axis=0, tiled=True)  54 us
    all_to_all x3, starting transfers between devices, cut_exchange(): lax.all_to_all(piece, axis, split_axis=0, concat_axis=0, tiled=True)  35.5 us
    all_to_all x1, blocking collectives, sent_to_all(): return lax.all_to_all(copies, axis, split_axis=0, concat_axis=0, tiled=True)  9.59 us
    all_to_all x1, blocking collectives, sent_and_summed(): parts = lax.all_to_all(cut_along(x, dim, devices), axis, 0, 0, tiled=True)  5.58 us
  transfers between devices with their start and end apart: 4, of which 3 were waited for; matrix products, arithmetic and copies ran while one was open for 4% of the time, Pallas kernels for 0%

commit v1 on v0

v1 whole, which is shorter than its diff:
```python
import functools

import jax
import jax.numpy as jnp
from jax import lax
from jax.experimental import pallas as pl
from jax.experimental.pallas import tpu as pltpu
from jax.sharding import PartitionSpec as P

MESH = pl.DeviceIdType.MESH
CAP = 5
NX = 4
STEPS = ((0, 8, 4, 12), (2, 14, 6, 10), (3, 13, 5, 11), (1, 15, 7, 9))
BF16 = jnp.bfloat16
F32 = jnp.float32
NT = (((1,), (1,)), ((), ()))
TN = (((0,), (0,)), ((), ()))


def kernel(
    steps, nx, routes, probs, grad_hbm, gate_pre_hbm, up_pre_hbm, gate_hbm, up_hbm, down_hbm, out,
    grad, gate_pre, up_pre, gate, up, down, spread, spread_in, select, sent, arrived, other,
    rows_own, rows_other, gate_mul, up_mul, grads, half_out, half_in, own_half, back, returned,
    total, local_sem, send_sem, recv_sem, pair_sem, y_send, y_recv, half_sem, back_send, back_recv,
):
    me, y, core = lax.axis_index("expert"), lax.axis_index("dp"), lax.axis_index("tensor")
    experts, n_dp = lax.axis_size("expert"), lax.axis_size("dp")
    nz = experts // nx
    z, x = me // nx, me % nx
    chunks, per = len(steps), len(steps[0]) * nx
    tokens, width = grad.shape
    blocks = width // 128
    message = sent.shape[2]
    hidden_width = gate.shape[1]
    deep = down_hbm.shape[0]
    tile = min(256, width)
    partner = {"tensor": 1 - core}
    ahead, behind = {"dp": lax.rem(y + 1, n_dp)}, {"dp": lax.rem(y + n_dp - 1, n_dp)}

    barrier = pltpu.get_barrier_semaphore()

    def greet(k, carry):
        pl.semaphore_signal(
            barrier, inc=1, device_id={"expert": lax.rem(me + k, experts)}, device_id_type=MESH
        )
        return carry

    lax.fori_loop(1, experts, greet, 0)
    for device in (partner, ahead, behind):
        pl.semaphore_signal(barrier, inc=1, device_id=device, device_id_type=MESH)

    own_rows = pl.ds(pl.multiple_of(y * deep, deep), deep)
    loads = [
        pltpu.make_async_copy(grad_hbm, grad, local_sem.at[0]),
        pltpu.make_async_copy(down_hbm, down.at[own_rows], local_sem.at[1]),
        pltpu.make_async_copy(gate_pre_hbm, gate_pre, local_sem.at[2]),
        pltpu.make_async_copy(up_pre_hbm, up_pre, local_sem.at[3]),
        pltpu.make_async_copy(gate_hbm, gate, local_sem.at[4]),
        pltpu.make_async_copy(up_hbm, up, local_sem.at[5]),
    ]
    for load in loads:
        load.start()

    def offsets(i):
        return [(dz, dx) for dz in steps[i] for dx in range(nx)]

    def toward(dz, dx):
        return {"expert": lax.rem(z + dz, nz) * nx + lax.rem(x + dx, nx)}

    def from_(dz, dx):
        return {"expert": lax.rem(z + nz - dz, nz) * nx + lax.rem(x + nx - dx, nx)}

    shift = nx.bit_length() - 1
    order = lax.broadcasted_iota(jnp.int32, (experts, tokens), 0)
    group = order >> shift
    dz_of = jnp.zeros_like(order)
    for j, dz in enumerate([dz for chunk in steps for dz in chunk]):
        dz_of = jnp.where(group == j, dz, dz_of)
    dx_of = order & (nx - 1)
    expert_of = ((dz_of + z) & (nz - 1)) * nx + ((dx_of + x) & (nx - 1))
    picked = jnp.zeros((experts, tokens), F32)
    weight = jnp.zeros((experts, tokens), F32)
    for k in range(routes.shape[0]):
        match = routes[k : k + 1, :] == expert_of
        picked = jnp.where(match, 1.0, picked)
        weight = jnp.where(match, probs[k : k + 1, :], weight)
    earlier = lax.broadcasted_iota(jnp.int32, (tokens, tokens), 0) < lax.broadcasted_iota(
        jnp.int32, (tokens, tokens), 1
    )
    before = jnp.dot(
        picked.astype(BF16), jnp.where(earlier, 1.0, 0.0).astype(BF16), preferred_element_type=F32
    )
    rank = jnp.where(picked > 0.5, before, -1.0)
    chosen = [jnp.where(jnp.abs(rank - r) < 0.5, 1.0, 0.0) for r in range(CAP)]
    spread[...] = jnp.zeros_like(spread)

    def put(value, r, block):
        spread[pl.ds(r * blocks + block, per, stride=message), :] = value

    def pack(destination):
        destination[...] = spread[...].reshape(per, message, 128).astype(BF16)

    def unpack(source, destination):
        spread_in[...] = source[...].astype(F32).reshape(per * message, 128)
        for r in range(CAP):
            for block in range(blocks):
                destination[r * per : (r + 1) * per, block * 128 : (block + 1) * 128] = spread_in[
                    pl.ds(r * blocks + block, per, stride=message), :
                ].astype(BF16)

    def dispatch_rows(i):
        part = slice(i * per, (i + 1) * per)
        table = jnp.concatenate([c[part] for c in chosen], axis=0)
        scale = jnp.sum(
            table * jnp.concatenate([weight[part]] * CAP, axis=0), axis=1, keepdims=True
        )
        select[i] = table.astype(BF16)
        for start in range(0, width, tile):
            rows = scale * jnp.dot(
                table.astype(BF16), grad[:, start : start + tile], preferred_element_type=F32
            )
            for r in range(CAP):
                for b in range(tile // 128):
                    put(
                        rows[r * per : (r + 1) * per, b * 128 : (b + 1) * 128],
                        r,
                        start // 128 + b,
                    )
        pack(sent.at[i])

    def exchange(i, source, target, device_of, s_sem, r_sem):
        for k, (dz, dx) in enumerate(offsets(i)):
            if dz == 0 and dx == 0:
                pltpu.make_async_copy(source.at[i, k], target.at[i, k], r_sem.at[i]).start()
            else:
                pltpu.make_async_remote_copy(
                    src_ref=source.at[i, k],
                    dst_ref=target.at[i, k],
                    send_sem=s_sem.at[i],
                    recv_sem=r_sem.at[i],
                    device_id=device_of(dz, dx),
                    device_id_type=MESH,
                ).start()

    def wait_arrival(i, target, r_sem):
        pltpu.make_async_copy(target.at[i], target.at[i], r_sem.at[i]).wait()

    def wait_sent(i, source, s_sem):
        first = 1 if offsets(i)[0] == (0, 0) else 0
        ref = source.at[i, pl.ds(first, per - first)]
        pltpu.make_async_copy(ref, ref, s_sem.at[i]).wait()

    def y_block(j):
        return down.at[pl.ds(pl.multiple_of(lax.rem(j + n_dp, n_dp) * deep, deep), deep)]

    def y_copies(s):
        copies = []
        if s < n_dp // 2:
            copies.append(
                pltpu.make_async_remote_copy(
                    src_ref=y_block(y - s), dst_ref=y_block(y - s), send_sem=y_send.at[0, s],
                    recv_sem=y_recv.at[0, s], device_id=ahead, device_id_type=MESH,
                )
            )
        if s < (n_dp - 1) // 2:
            copies.append(
                pltpu.make_async_remote_copy(
                    src_ref=y_block(y + s), dst_ref=y_block(y + s), send_sem=y_send.at[1, s],
                    recv_sem=y_recv.at[1, s], device_id=behind, device_id_type=MESH,
                )
            )
        return copies

    def y_wait(s):
        if s < n_dp // 2:
            pltpu.make_async_copy(
                y_block(y - 1 - s), y_block(y - 1 - s), y_recv.at[0, s]
            ).wait()
        if s < (n_dp - 1) // 2:
            pltpu.make_async_copy(
                y_block(y + 1 + s), y_block(y + 1 + s), y_recv.at[1, s]
            ).wait()

    def y_step(s):
        if s < n_dp // 2:
            y_wait(s)
            for copy in y_copies(s + 1):
                copy.start()

    def pair_copy(i):
        return pltpu.make_async_remote_copy(
            src_ref=arrived.at[i], dst_ref=other.at[i], send_sem=pair_sem.at[0, i],
            recv_sem=pair_sem.at[1, i], device_id=partner, device_id_type=MESH,
        )

    def half_copy(i):
        return pltpu.make_async_remote_copy(
            src_ref=half_out.at[i], dst_ref=half_in.at[i], send_sem=half_sem.at[0, i],
            recv_sem=half_sem.at[1, i], device_id=partner, device_id_type=MESH,
        )

    def factors(i):
        row = lax.broadcasted_iota(jnp.int32, (CAP * per, 1), 0)
        r_of = jnp.zeros_like(row)
        for r in range(1, CAP):
            r_of = jnp.where(row >= r * per, r, r_of)
        k_of = row - r_of * per
        dz_row = jnp.zeros_like(row)
        for j, dz in enumerate(steps[i]):
            dz_row = jnp.where((k_of >> shift) == j, dz, dz_row)
        source = ((z + nz - dz_row) & (nz - 1)) * nx + ((x + nx - (k_of & (nx - 1))) & (nx - 1))
        place = jnp.where(
            lax.broadcasted_iota(jnp.int32, (CAP * per, experts * CAP), 1) == source * CAP + r_of,
            1.0,
            0.0,
        ).astype(BF16)
        a = jnp.dot(place, gate_pre[...], preferred_element_type=F32)
        b = jnp.dot(place, up_pre[...], preferred_element_type=F32)
        q = jax.nn.sigmoid(a)
        gate_mul[i] = b * (q * (1.0 + a * (1.0 - q)))
        up_mul[i] = a * q

    def take(i):
        wait_arrival(i, arrived, recv_sem)
        pair_copy(i).start()
        unpack(arrived.at[i], rows_own.at[i])

    def half_rows(half, start):
        return pl.ds(pl.multiple_of(half * width + start, tile), tile)

    def partial(half, start):
        rows = half_rows(half, start)
        return lax.dot_general(
            grads[0], gate[rows, :], NT, preferred_element_type=F32
        ) + lax.dot_general(grads[1], up[rows, :], NT, preferred_element_type=F32)

    def work(i):
        pair_copy(i).wait()
        unpack(other.at[i], rows_other)
        own_down = down[pl.ds(pl.multiple_of(core * width, width), width), :]
        other_down = down[pl.ds(pl.multiple_of((1 - core) * width, width), width), :]
        hidden = jnp.dot(rows_own[i], own_down, preferred_element_type=F32) + jnp.dot(
            rows_other[...], other_down, preferred_element_type=F32
        )
        grads[0] = (hidden * gate_mul[i]).astype(BF16)
        grads[1] = (hidden * up_mul[i]).astype(BF16)
        for start in range(0, width, tile):
            half_out[i, :, start : start + tile] = partial(1 - core, start).astype(BF16)
        half_copy(i).start()
        for start in range(0, width, tile):
            own_half[:, start : start + tile] = partial(core, start).astype(BF16)
        half_copy(i).wait()
        for r in range(CAP):
            for block in range(blocks):
                at = (slice(r * per, (r + 1) * per), slice(block * 128, (block + 1) * 128))
                put(own_half[at].astype(F32) + half_in[(i,) + at].astype(F32), r, block)
        pack(back.at[i])
        exchange(i, back, returned, from_, back_send, back_recv)

    def gather(i):
        wait_arrival(i, returned, back_recv)
        unpack(returned.at[i], rows_other)
        for start in range(0, width, tile):
            cols = slice(start, start + tile)
            value = lax.dot_general(select[i], rows_other[:, cols], TN, preferred_element_type=F32)
            if i > 0:
                value = value + total[:, cols]
            if i == chunks - 1:
                out[:, cols] = value.astype(BF16)
            else:
                total[:, cols] = value

    loads[0].wait()
    dispatch_rows(0)
    pl.semaphore_wait(barrier, experts + 2)
    exchange(0, sent, arrived, toward, send_sem, recv_sem)
    loads[1].wait()
    for copy in y_copies(0):
        copy.start()
    for i in range(1, chunks):
        dispatch_rows(i)
        exchange(i, sent, arrived, toward, send_sem, recv_sem)
    loads[2].wait()
    loads[3].wait()
    for i in range(chunks):
        factors(i)
    loads[4].wait()
    loads[5].wait()
    y_step(0)
    take(0)
    y_step(1)
    if chunks > 1:
        take(1)
    for s in range(2, n_dp // 2):
        y_step(s)
    work(0)
    if chunks > 1:
        work(1)
    for i in range(2, chunks):
        take(i)
        work(i)
    for i in range(chunks):
        gather(i)
    for i in range(chunks):
        wait_sent(i, sent, send_sem)
        wait_sent(i, back, back_send)
    for s in range(n_dp // 2):
        for copy in y_copies(s):
            copy.wait_send()


def local(steps, nx, out_grad, routes, probs, gate_pre, up_pre, gate, up, down):
    tokens, width = out_grad.shape
    slots, hidden = gate_pre.shape[2:]
    full = gate.shape[1]
    chunks, per = len(steps), len(steps[0]) * nx
    message = -(-CAP * (width // 128) // 8) * 8
    n_dp = lax.axis_size("dp")
    experts = lax.axis_size("expert")
    flight = pltpu.VMEM((chunks, per, message, 128), BF16)
    rows = CAP * per
    dma = pltpu.SemaphoreType.DMA
    anywhere = pl.BlockSpec(memory_space=pl.ANY)
    vmem = pl.BlockSpec(memory_space=pltpu.VMEM)
    return pl.pallas_call(
        functools.partial(kernel, steps, nx),
        out_shape=jax.ShapeDtypeStruct((tokens, width), BF16),
        in_specs=[vmem] * 2 + [anywhere] * 6,
        out_specs=vmem,
        scratch_shapes=[
            pltpu.VMEM((tokens, width), BF16),
            pltpu.VMEM((slots, hidden), BF16),
            pltpu.VMEM((slots, hidden), BF16),
            pltpu.VMEM((full, hidden), BF16),
            pltpu.VMEM((full, hidden), BF16),
            pltpu.VMEM((full, hidden), BF16),
            pltpu.VMEM((per * message, 128), F32),
            pltpu.VMEM((per * message, 128), F32),
            pltpu.VMEM((chunks, rows, tokens), BF16),
            flight,
            flight,
            flight,
            pltpu.VMEM((chunks, rows, width), BF16),
            pltpu.VMEM((rows, width), BF16),
            pltpu.VMEM((chunks, rows, hidden), F32),
            pltpu.VMEM((chunks, rows, hidden), F32),
            pltpu.VMEM((2, rows, hidden), BF16),
            pltpu.VMEM((chunks, rows, width), BF16),
            pltpu.VMEM((chunks, rows, width), BF16),
            pltpu.VMEM((rows, width), BF16),
            flight,
            flight,
            pltpu.VMEM((tokens, width), F32),
            dma((6,)),
            dma((chunks,)),
            dma((chunks,)),
            dma((2, chunks)),
            dma((2, n_dp // 2)),
            dma((2, n_dp // 2)),
            dma((2, chunks)),
            dma((chunks,)),
            dma((chunks,)),
        ],
        compiler_params=pltpu.CompilerParams(
            collective_id=0, has_side_effects=True, vmem_limit_bytes=60 * 1024 * 1024
        ),
    )(
        routes.T, probs.T, out_grad, gate_pre[0, 0], up_pre[0, 0], gate[0], up[0], down[0].T
    )


def solution(mesh):
    placed = (
        P(("dp", "expert"), "tensor"),
        P(("dp", "expert"), None),
        P(("dp", "expert"), None),
        P("dp", "expert", None, "tensor"),
        P("dp", "expert", None, "tensor"),
        P("expert", None, "tensor"),
        P("expert", None, "tensor"),
        P("expert", "tensor", "dp"),
    )
    return jax.shard_map(
        functools.partial(local, STEPS, NX),
        mesh=mesh,
        in_specs=placed,
        out_specs=P(("dp", "expert"), "tensor"),
        check_vma=False,
    )
```

time: 247 us -> 136 us (0.55); the launches traced: 244 us -> 135 us
  Pallas kernels: 0 us -> 134 us
  waiting for transfers between devices: 100 us -> 0 us
  blocking collectives: 69.1 us -> 0 us
  starting transfers between devices: 35.5 us -> 0 us
  between operations: 13.7 us -> 0.01 us
  matrix products: 8.17 us -> 0 us
  local copies, waits for them, and re-layouts: 9.49 us -> 1.82 us
  other arithmetic: 7.41 us -> 0 us
    pallas_call x0 -> x1, Pallas kernels: none -> 134 us  [local(): pl.pallas_call(functools.partial(kernel, steps, nx), out_shape=jax.ShapeD...]
    all_to_all x3 -> x0, waiting for transfers between devices: 99.6 us -> none  [cut_exchange(): lax.all_to_all(piece, axis, split_axis=0, concat_axis=0, tiled=True)]
    all_to_all x3 -> x0, blocking collectives: 69.1 us -> none  [the longest x1 54 us: cut_exchange(): lax.all_to_all(piece, axis, split_axis=0, concat_axis=0, tiled=True)]
    all_to_all x3 -> x0, starting transfers between devices: 35.5 us -> none  [cut_exchange(): lax.all_to_all(piece, axis, split_axis=0, concat_axis=0, tiled=True)]
    dot_general x5 -> x0, matrix products: 8.17 us -> none  [the longest x1 3.53 us: local(): lax.dot_general(gathered, lax.all_gather(down_local, 'dp', axis=1, tiled=...]
    split x4 -> x0, local copies, waits for them, and re-layouts: 4.06 us -> none  [cut_exchange(): jnp.split(parts, cut_rows(parts.shape[split_at], pieces), axis=split_at)]
    concatenate x2 -> x0, other arithmetic: 3.83 us -> none  [cut_exchange(): return in_order(jnp.concatenate(outs, axis=split_at), concat_dim)]
    another operation x4 -> x0, local copies, waits for them, and re-layouts: 3.81 us -> none  [the longest x2 2.77 us: cut_along(): return jnp.moveaxis(x.reshape(*before, devices, -1, *after), dim, 0)]
  transfers between devices with their start and end apart: 4 -> 0, of which waited for: 3 -> 0; matrix products, arithmetic and copies ran while one was open for 4% -> 0% of each run, Pallas kernels for 0% -> 0%
where the time goes in v1:
time: 136 us; the launch traced here: 135 us
  Pallas kernels  134 us (99%)
  local copies, waits for them, and re-layouts  1.82 us (1%)
    pallas_call x1, Pallas kernels, local(): pl.pallas_call(functools.partial(kernel, steps, nx), out_shape=jax.ShapeD...  134 us

profile of v1, /device:TPU:1, one launch (start us, length us, event | category | flops | bytes accessed | tf_op | source)
XLA Modules:
  0.0 135.4 jit_solution(8610240746780613189)
XLA Ops:
  0.0 133.5 %shard_map.82 = bf16[128,1792]{1,0:T(8,128)(2,1)} custom-call(s32[8,128]{1,0:T(8,128)} %bitcast.14, f32[8,128]{1,0:T(8,128)} %bitcast.15, bf16[128,1792]{1,0:T(8,128)(2,1)} %grad_hbm.1, bf16[320,512]{1,0:T(8,128)(2,1)} %bitcast.12, bf16[320,512]{1,0:T(8,128)(2,1)} %bitcast.13, bf16[3584,512]{1,0:T(8,128)(2,1)} %bitcast.9, bf16[3584,512]{1,0:T(8,128)(2,1)} %bitcast.10, ...), custom_call_target="tpu_custom_call" | custom-call | tf_op jit(solution)/shard_map/pallas_call | solution.py:325
  133.5 1.8 %copy.10 = bf16[128,1792]{1,0:T(8,128)(2,1)} copy(bf16[128,1792]{1,0:T(8,128)(2,1)} %shard_map.82) | data formatting | bytes 917504

commit v2 on v1

--- a/solution.py
+++ b/solution.py
@@ -10,7 +10,7 @@
 MESH = pl.DeviceIdType.MESH
 CAP = 5
 NX = 4
-STEPS = ((0, 8, 4, 12), (2, 14, 6, 10), (3, 13, 5, 11), (1, 15, 7, 9))
+STEPS = ((0, 8, 9, 7), (10, 6, 11, 5), (12, 4, 13, 3), (14, 2, 15, 1))
 BF16 = jnp.bfloat16
 F32 = jnp.float32
 NT = (((1,), (1,)), ((), ()))
@@ -39,13 +39,14 @@
 
     barrier = pltpu.get_barrier_semaphore()
 
-    def greet(k, carry):
+    def greet(j, carry):
+        k = experts // 2 + (1 - 2 * (j % 2)) * ((j + 1) // 2)
         pl.semaphore_signal(
             barrier, inc=1, device_id={"expert": lax.rem(me + k, experts)}, device_id_type=MESH
         )
         return carry
 
-    lax.fori_loop(1, experts, greet, 0)
+    lax.fori_loop(0, experts - 1, greet, 0)
     for device in (partner, ahead, behind):
         pl.semaphore_signal(barrier, inc=1, device_id=device, device_id_type=MESH)
 
@@ -150,41 +151,30 @@
         ref = source.at[i, pl.ds(first, per - first)]
         pltpu.make_async_copy(ref, ref, s_sem.at[i]).wait()
 
-    def y_block(j):
-        return down.at[pl.ds(pl.multiple_of(lax.rem(j + n_dp, n_dp) * deep, deep), deep)]
-
-    def y_copies(s):
+    def y_part(j, half):
+        start = lax.rem(j + n_dp, n_dp) * deep + half * (deep // 2)
+        return down.at[pl.ds(pl.multiple_of(start, deep // 2), deep // 2)]
+
+    y_steps = n_dp - 1
+
+    def y_copies(m):
+        s, half = m // 2, m % 2
         copies = []
-        if s < n_dp // 2:
+        for way, (j, h, device) in enumerate(((y - s, half, ahead), (y + s, 1 - half, behind))):
             copies.append(
                 pltpu.make_async_remote_copy(
-                    src_ref=y_block(y - s), dst_ref=y_block(y - s), send_sem=y_send.at[0, s],
-                    recv_sem=y_recv.at[0, s], device_id=ahead, device_id_type=MESH,
-                )
-            )
-        if s < (n_dp - 1) // 2:
-            copies.append(
-                pltpu.make_async_remote_copy(
-                    src_ref=y_block(y + s), dst_ref=y_block(y + s), send_sem=y_send.at[1, s],
-                    recv_sem=y_recv.at[1, s], device_id=behind, device_id_type=MESH,
+                    src_ref=y_part(j, h), dst_ref=y_part(j, h), send_sem=y_send.at[way, m],
+                    recv_sem=y_recv.at[way, m], device_id=device, device_id_type=MESH,
                 )
             )
         return copies
 
-    def y_wait(s):
-        if s < n_dp // 2:
-            pltpu.make_async_copy(
-                y_block(y - 1 - s), y_block(y - 1 - s), y_recv.at[0, s]
-            ).wait()
-        if s < (n_dp - 1) // 2:
-            pltpu.make_async_copy(
-                y_block(y + 1 + s), y_block(y + 1 + s), y_recv.at[1, s]
-            ).wait()
-
-    def y_step(s):
-        if s < n_dp // 2:
-            y_wait(s)
-            for copy in y_copies(s + 1):
+    def y_step(m):
+        s, half = m // 2, m % 2
+        for way, (j, h) in enumerate(((y - 1 - s, half), (y + 1 + s, 1 - half))):
+            pltpu.make_async_copy(y_part(j, h), y_part(j, h), y_recv.at[way, m]).wait()
+        if m + 2 < y_steps:
+            for copy in y_copies(m + 2):
                 copy.start()
 
     def pair_copy(i):
@@ -275,24 +265,27 @@
     pl.semaphore_wait(barrier, experts + 2)
     exchange(0, sent, arrived, toward, send_sem, recv_sem)
     loads[1].wait()
-    for copy in y_copies(0):
-        copy.start()
+    for m in range(min(2, y_steps)):
+        for copy in y_copies(m):
+            copy.start()
     for i in range(1, chunks):
         dispatch_rows(i)
         exchange(i, sent, arrived, toward, send_sem, recv_sem)
     loads[2].wait()
     loads[3].wait()
+    for m in range(0, min(1, y_steps)):
+        y_step(m)
     for i in range(chunks):
         factors(i)
+    for m in range(1, min(4, y_steps)):
+        y_step(m)
+    take(0)
+    for m in range(4, y_steps):
+        y_step(m)
     loads[4].wait()
     loads[5].wait()
-    y_step(0)
-    take(0)
-    y_step(1)
     if chunks > 1:
         take(1)
-    for s in range(2, n_dp // 2):
-        y_step(s)
     work(0)
     if chunks > 1:
         work(1)
@@ -304,8 +297,8 @@
     for i in range(chunks):
         wait_sent(i, sent, send_sem)
         wait_sent(i, back, back_send)
-    for s in range(n_dp // 2):
-        for copy in y_copies(s):
+    for m in range(y_steps):
+        for copy in y_copies(m):
             copy.wait_send()
 
 
@@ -355,8 +348,8 @@
             dma((chunks,)),
             dma((chunks,)),
             dma((2, chunks)),
-            dma((2, n_dp // 2)),
-            dma((2, n_dp // 2)),
+            dma((2, n_dp - 1)),
+            dma((2, n_dp - 1)),
             dma((2, chunks)),
             dma((chunks,)),
             dma((chunks,)),

time: 136 us -> 131 us (0.963)
  Pallas kernels: 134 us -> 129 us
    pallas_call x1, Pallas kernels: 134 us -> 129 us  [local(): pl.pallas_call(functools.partial(kernel, steps, nx), out_shape=jax.ShapeD...]
where the time goes in v2:
time: 131 us
  Pallas kernels  129 us (98%)
  local copies, waits for them, and re-layouts  1.82 us (1%)
    pallas_call x1, Pallas kernels, local(): pl.pallas_call(functools.partial(kernel, steps, nx), out_shape=jax.ShapeD...  129 us

profile of v2, /device:TPU:1, one launch (start us, length us, event | category | flops | bytes accessed | tf_op | source)
XLA Modules:
  0.0 130.8 jit_solution(1971438954577206192)
XLA Ops:
  0.0 129.0 %shard_map.82 = bf16[128,1792]{1,0:T(8,128)(2,1)} custom-call(s32[8,128]{1,0:T(8,128)} %bitcast.14, f32[8,128]{1,0:T(8,128)} %bitcast.15, bf16[128,1792]{1,0:T(8,128)(2,1)} %grad_hbm.1, bf16[320,512]{1,0:T(8,128)(2,1)} %bitcast.12, bf16[320,512]{1,0:T(8,128)(2,1)} %bitcast.13, bf16[3584,512]{1,0:T(8,128)(2,1)} %bitcast.9, bf16[3584,512]{1,0:T(8,128)(2,1)} %bitcast.10, ...), custom_call_target="tpu_custom_call" | custom-call | tf_op jit(solution)/shard_map/pallas_call | solution.py:318
  129.0 1.8 %copy.10 = bf16[128,1792]{1,0:T(8,128)(2,1)} copy(bf16[128,1792]{1,0:T(8,128)(2,1)} %shard_map.82) | data formatting | bytes 917504

commit v3 on v2

--- a/solution.py
+++ b/solution.py
@@ -11,6 +11,7 @@
 CAP = 5
 NX = 4
 STEPS = ((0, 8, 9, 7), (10, 6, 11, 5), (12, 4, 13, 3), (14, 2, 15, 1))
+NEAR = 2
 BF16 = jnp.bfloat16
 F32 = jnp.float32
 NT = (((1,), (1,)), ((), ()))
@@ -22,6 +23,7 @@
     grad, gate_pre, up_pre, gate, up, down, spread, spread_in, select, sent, arrived, other,
     rows_own, rows_other, gate_mul, up_mul, grads, half_out, half_in, own_half, back, returned,
     total, local_sem, send_sem, recv_sem, pair_sem, y_send, y_recv, half_sem, back_send, back_recv,
+    round_sem,
 ):
     me, y, core = lax.axis_index("expert"), lax.axis_index("dp"), lax.axis_index("tensor")
     experts, n_dp = lax.axis_size("expert"), lax.axis_size("dp")
@@ -39,16 +41,29 @@
 
     barrier = pltpu.get_barrier_semaphore()
 
-    def greet(j, carry):
-        k = experts // 2 + (1 - 2 * (j % 2)) * ((j + 1) // 2)
-        pl.semaphore_signal(
-            barrier, inc=1, device_id={"expert": lax.rem(me + k, experts)}, device_id_type=MESH
-        )
-        return carry
-
-    lax.fori_loop(0, experts - 1, greet, 0)
+    def toward(dz, dx):
+        return {"expert": lax.rem(z + dz, nz) * nx + lax.rem(x + dx, nx)}
+
+    def from_(dz, dx):
+        return {"expert": lax.rem(z + nz - dz, nz) * nx + lax.rem(x + nx - dx, nx)}
+
+    near_rows = sorted({dz % nz for dz in range(-NEAR, NEAR + 1)}, key=lambda dz: -min(dz, nz - dz))
+    greeted = [(dz, dx) for dz in near_rows for dx in range(nx) if (dz, dx) != (0, 0)]
+    for dz, dx in greeted:
+        pl.semaphore_signal(barrier, inc=1, device_id=toward(dz, dx), device_id_type=MESH)
     for device in (partner, ahead, behind):
         pl.semaphore_signal(barrier, inc=1, device_id=device, device_id_type=MESH)
+
+    def tell(n):
+        step = NEAR << n
+        for dz in (step, nz - step):
+            pl.semaphore_signal(
+                round_sem.at[n], inc=1, device_id=toward(dz, 0), device_id_type=MESH
+            )
+
+    rounds = 0
+    while NEAR << rounds < nz // 2:
+        rounds += 1
 
     own_rows = pl.ds(pl.multiple_of(y * deep, deep), deep)
     loads = [
@@ -64,12 +79,6 @@
 
     def offsets(i):
         return [(dz, dx) for dz in steps[i] for dx in range(nx)]
-
-    def toward(dz, dx):
-        return {"expert": lax.rem(z + dz, nz) * nx + lax.rem(x + dx, nx)}
-
-    def from_(dz, dx):
-        return {"expert": lax.rem(z + nz - dz, nz) * nx + lax.rem(x + nx - dx, nx)}
 
     shift = nx.bit_length() - 1
     order = lax.broadcasted_iota(jnp.int32, (experts, tokens), 0)
@@ -260,16 +269,24 @@
             else:
                 total[:, cols] = value
 
+    near = chunks - 1
     loads[0].wait()
-    dispatch_rows(0)
-    pl.semaphore_wait(barrier, experts + 2)
-    exchange(0, sent, arrived, toward, send_sem, recv_sem)
+    dispatch_rows(near)
+    pl.semaphore_wait(barrier, len(greeted) + 3)
+    if rounds:
+        tell(0)
+    exchange(near, sent, arrived, toward, send_sem, recv_sem)
     loads[1].wait()
     for m in range(min(2, y_steps)):
         for copy in y_copies(m):
             copy.start()
-    for i in range(1, chunks):
+    for n in range(1, rounds):
+        pl.semaphore_wait(round_sem.at[n - 1], 2)
+        tell(n)
+    for i in range(near):
         dispatch_rows(i)
+        if i == 0 and rounds:
+            pl.semaphore_wait(round_sem.at[rounds - 1], 2)
         exchange(i, sent, arrived, toward, send_sem, recv_sem)
     loads[2].wait()
     loads[3].wait()
@@ -279,19 +296,21 @@
         factors(i)
     for m in range(1, min(4, y_steps)):
         y_step(m)
-    take(0)
+    take(near)
+    if near > 0:
+        take(0)
     for m in range(4, y_steps):
         y_step(m)
     loads[4].wait()
     loads[5].wait()
-    if chunks > 1:
+    if near > 1:
         take(1)
-    work(0)
-    if chunks > 1:
-        work(1)
-    for i in range(2, chunks):
+    for i in range(min(2, near)):
+        work(i)
+    for i in range(2, near):
         take(i)
         work(i)
+    work(near)
     for i in range(chunks):
         gather(i)
     for i in range(chunks):
@@ -353,6 +372,7 @@
             dma((2, chunks)),
             dma((chunks,)),
             dma((chunks,)),
+            pltpu.SemaphoreType.REGULAR((4,)),
         ],
         compiler_params=pltpu.CompilerParams(
             collective_id=0, has_side_effects=True, vmem_limit_bytes=60 * 1024 * 1024

time: 131 us -> 130 us (level)
  Pallas kernels: 129 us -> 127 us
    pallas_call x1, Pallas kernels: 129 us -> 127 us  [local(): pl.pallas_call(functools.partial(kernel, steps, nx), out_shape=jax.ShapeD...]
where the time goes in v3:
time: 130 us; the launch traced here: 129 us
  Pallas kernels  127 us (98%)
  local copies, waits for them, and re-layouts  1.82 us (1%)
    pallas_call x1, Pallas kernels, local(): pl.pallas_call(functools.partial(kernel, steps, nx), out_shape=jax.ShapeD...  127 us

profile of v3, /device:TPU:1, one launch (start us, length us, event | category | flops | bytes accessed | tf_op | source)
XLA Modules:
  0.0 129.3 jit_solution(7352359023872095550)
XLA Ops:
  0.0 127.5 %shard_map.82 = bf16[128,1792]{1,0:T(8,128)(2,1)} custom-call(s32[8,128]{1,0:T(8,128)} %bitcast.14, f32[8,128]{1,0:T(8,128)} %bitcast.15, bf16[128,1792]{1,0:T(8,128)(2,1)} %grad_hbm.1, bf16[320,512]{1,0:T(8,128)(2,1)} %bitcast.12, bf16[320,512]{1,0:T(8,128)(2,1)} %bitcast.13, bf16[3584,512]{1,0:T(8,128)(2,1)} %bitcast.9, bf16[3584,512]{1,0:T(8,128)(2,1)} %bitcast.10, ...), custom_call_target="tpu_custom_call" | custom-call | tf_op jit(solution)/shard_map/pallas_call | solution.py:337
  127.5 1.8 %copy.10 = bf16[128,1792]{1,0:T(8,128)(2,1)} copy(bf16[128,1792]{1,0:T(8,128)(2,1)} %shard_map.82) | data formatting | bytes 917504

commit v4 on v3

--- a/solution.py
+++ b/solution.py
@@ -15,7 +15,6 @@
 BF16 = jnp.bfloat16
 F32 = jnp.float32
 NT = (((1,), (1,)), ((), ()))
-TN = (((0,), (0,)), ((), ()))
 
 
 def kernel(
@@ -23,7 +22,7 @@
     grad, gate_pre, up_pre, gate, up, down, spread, spread_in, select, sent, arrived, other,
     rows_own, rows_other, gate_mul, up_mul, grads, half_out, half_in, own_half, back, returned,
     total, local_sem, send_sem, recv_sem, pair_sem, y_send, y_recv, half_sem, back_send, back_recv,
-    round_sem,
+    round_sem, select_t, combined, out_sem,
 ):
     me, y, core = lax.axis_index("expert"), lax.axis_index("dp"), lax.axis_index("tensor")
     experts, n_dp = lax.axis_size("expert"), lax.axis_size("dp")
@@ -102,7 +101,8 @@
     )
     rank = jnp.where(picked > 0.5, before, -1.0)
     chosen = [jnp.where(jnp.abs(rank - r) < 0.5, 1.0, 0.0) for r in range(CAP)]
-    spread[...] = jnp.zeros_like(spread)
+    for row in range(CAP * blocks, message):
+        spread[pl.ds(row, per, stride=message), :] = jnp.zeros((per, 128), F32)
 
     def put(value, r, block):
         spread[pl.ds(r * blocks + block, per, stride=message), :] = value
@@ -216,6 +216,7 @@
         a = jnp.dot(place, gate_pre[...], preferred_element_type=F32)
         b = jnp.dot(place, up_pre[...], preferred_element_type=F32)
         q = jax.nn.sigmoid(a)
+        select_t[i] = jnp.transpose(select[i].astype(F32)).astype(BF16)
         gate_mul[i] = b * (q * (1.0 + a * (1.0 - q)))
         up_mul[i] = a * q
 
@@ -259,15 +260,20 @@
     def gather(i):
         wait_arrival(i, returned, back_recv)
         unpack(returned.at[i], rows_other)
-        for start in range(0, width, tile):
+        for n, start in enumerate(range(0, width, tile)):
             cols = slice(start, start + tile)
-            value = lax.dot_general(select[i], rows_other[:, cols], TN, preferred_element_type=F32)
+            value = jnp.dot(select_t[i], rows_other[:, cols], preferred_element_type=F32)
             if i > 0:
                 value = value + total[:, cols]
             if i == chunks - 1:
-                out[:, cols] = value.astype(BF16)
+                combined[:, cols] = value.astype(BF16)
+                out_copy(n).start()
             else:
                 total[:, cols] = value
+
+    def out_copy(n):
+        cols = slice(n * tile, (n + 1) * tile)
+        return pltpu.make_async_copy(combined.at[:, cols], out.at[:, cols], out_sem.at[n])
 
     near = chunks - 1
     loads[0].wait()
@@ -313,6 +319,8 @@
     work(near)
     for i in range(chunks):
         gather(i)
+    for n in range(width // tile):
+        out_copy(n).wait()
     for i in range(chunks):
         wait_sent(i, sent, send_sem)
         wait_sent(i, back, back_send)
@@ -338,7 +346,7 @@
         functools.partial(kernel, steps, nx),
         out_shape=jax.ShapeDtypeStruct((tokens, width), BF16),
         in_specs=[vmem] * 2 + [anywhere] * 6,
-        out_specs=vmem,
+        out_specs=anywhere,
         scratch_shapes=[
             pltpu.VMEM((tokens, width), BF16),
             pltpu.VMEM((slots, hidden), BF16),
@@ -373,6 +381,9 @@
             dma((chunks,)),
             dma((chunks,)),
             pltpu.SemaphoreType.REGULAR((4,)),
+            pltpu.VMEM((chunks, tokens, rows), BF16),
+            pltpu.VMEM((tokens, width), BF16),
+            dma((-(-width // 256),)),
         ],
         compiler_params=pltpu.CompilerParams(
             collective_id=0, has_side_effects=True, vmem_limit_bytes=60 * 1024 * 1024

time: 130 us -> 129 us (level)
  no operation moved by 1% of the time
where the time goes in v4:
time: 129 us
  Pallas kernels  127 us (98%)
  local copies, waits for them, and re-layouts  1.82 us (1%)
    pallas_call x1, Pallas kernels, local(): pl.pallas_call(functools.partial(kernel, steps, nx), out_shape=jax.ShapeD...  127 us

profile of v4, /device:TPU:1, one launch (start us, length us, event | category | flops | bytes accessed | tf_op | source)
XLA Modules:
  0.0 129.3 jit_solution(6346291153715149607)
XLA Ops:
  0.0 127.4 %shard_map.82 = bf16[128,1792]{1,0:T(8,128)(2,1)} custom-call(s32[8,128]{1,0:T(8,128)} %bitcast.14, f32[8,128]{1,0:T(8,128)} %bitcast.15, bf16[128,1792]{1,0:T(8,128)(2,1)} %grad_hbm.1, bf16[320,512]{1,0:T(8,128)(2,1)} %bitcast.12, bf16[320,512]{1,0:T(8,128)(2,1)} %bitcast.13, bf16[3584,512]{1,0:T(8,128)(2,1)} %bitcast.9, bf16[3584,512]{1,0:T(8,128)(2,1)} %bitcast.10, ...), custom_call_target="tpu_custom_call" | custom-call | tf_op jit(solution)/shard_map/pallas_call | solution.py:345
  127.4 1.8 %copy.10 = bf16[128,1792]{1,0:T(8,128)(2,1)} copy(bf16[128,1792]{1,0:T(8,128)(2,1)} %shard_map.82) | data formatting | bytes 917504
